TPU v7x, 512 devices: a whole 4x8x8 slice. The times are simulated.
512 devices in a mesh: grp: 16 (over y, z_lo), col: 32 (over x, z_hi, core).
Axes of the slice: x: 4, y: 8, z: 8 (z_hi: 4, z_lo: 2; z = z_hi * 2 + z_lo), core: 2. Of those that a mesh axis runs over, the one named last changes fastest.
Arguments:
- border: bfloat16 [64, 384, 24576], P('grp', None, 'col'), may hold values from -0.30859375 to 0.30859375
- inverses: bfloat16 [64, 384, 384], P('grp'), may hold values from -0.3125 to 0.3125
- scen_map: int32 [16, 4], P('grp'), may hold values from 0 to 3, each once within a row
- owners: int32 [4], replicated, may hold values from 0 to 31
- slots: int32 [4], replicated, may hold values from 0 to 2
Outputs:
- schur_cols: float32 [4, 24576, 256], P(None, ('col', 'grp'))
All inputs are finite; a program needn't handle non-finite values.
Results may differ from a plain program's by a relative error of at most 0.0029.
Values may be sent and summed in bfloat16 or wider, within the bound.
A program may use at most 64 MiB of HBM per device.

v0:
```python
import jax
import jax.numpy as jnp
from jax import lax
from jax.sharding import PartitionSpec as P

PW = 256


def spread(block, axis, holder):
    block = jnp.where(lax.axis_index(axis) == holder, block, jnp.zeros_like(block))
    return lax.psum(block, axis)


def apply_panel(border, chosen, slot):
    panel = lax.dynamic_slice_in_dim(border, slot * PW, PW, 2)
    return jnp.einsum("sij,sjc->sic", chosen, panel, preferred_element_type=jnp.float32).astype(
        jnp.bfloat16
    )


def share_panel(border, chosen, slot, owner):
    applied = apply_panel(border, chosen, slot)
    return spread(applied, "col", owner)


def on_device(border, inverses, scen_map, owners, slots):
    chosen = jnp.take(inverses, scen_map[0], axis=0)
    panels = owners.shape[0]
    partials = []
    for p in range(panels):
        shared = share_panel(border, chosen, slots[p], owners[p])
        partials.append(
            jnp.einsum("sir,sic->rc", border, shared, preferred_element_type=jnp.float32)
        )
    results = []
    for p in range(panels):
        results.append(lax.psum_scatter(partials[p], "grp", scatter_dimension=0, tiled=True))
    return jnp.stack(results)


def solution(mesh):
    return jax.shard_map(
        on_device,
        mesh=mesh,
        in_specs=(P("grp", None, "col"), P("grp", None, None), P("grp", None), P(), P()),
        out_specs=P(None, ("col", "grp"), None),
        check_vma=False,
    )
```

profile of v0, /device:TPU:6, one launch (start us, length us, event | category | flops | bytes accessed | tf_op | source)
XLA Modules:
  0.0 637.8 jit_solution(4205355091439734565)
XLA Ops:
  6.5 0.8 compare_and_fusion
  7.4 0.7 fusion.12
  8.0 1.5 fusion.14
  12.1 1.5 fusion.13
  16.1 2.1 gather_fusion
  18.2 1.7 fusion.1
  19.9 1.7 fusion.2
  21.6 1.7 fusion.3
  23.2 1.7 fusion
  24.9 0.0 reduce-scatter.19.cloned.1.call-start
  25.0 292.9 %all-reduce.3.cloned.1.call-done = (bf16[4,384,256]{1,2,0:T(8,128)(2,1)}, bf16[4,384,256]{1,2,0:T(8,128)(2,1)}, bf16[4,384,256]{1,2,0:T(8,128)(2,1)}, bf16[4,384,256]{1,2,0:T(8,128)(2,1)}) async-done(((bf16[4,384,256]{1,2,0:T(8,128)(2,1)}, bf16[4,384,256]{1,2,0:T(8,128)(2,1)}, bf16[4,384,256]{1,2,0:T(8,128)(2,1)}, bf16[4,384,256]{1,2,0:T(8,128)(2,1)}), (bf16[4,384,256]{1,2,0:T(8,128)(2,1)}, ...) | async-done | bytes 3145744 | tf_op jit(solution)/shard_map/psum | solution.py:11
  317.9 1.9 convolution_bitcast_fusion
  319.8 1.2 copy.17
  321.0 1.9 convolution_bitcast_fusion.1
  322.9 1.2 copy.15
  324.1 1.9 convolution_bitcast_fusion.3
  326.1 1.2 copy.11
  327.3 1.9 convolution_bitcast_fusion.2
  329.2 1.2 copy.13
  330.4 75.3 %reduce-scatter.19.cloned.1.call-done = f32[48,256]{1,0:T(8,128)} async-done(((f32[768,256]{1,0:T(8,128)}), f32[48,256]{1,0:T(8,128)}) %reduce-scatter.19.cloned.1.call-update) | async-done | bytes 49168
  405.7 0.9 copy.18
  406.6 0.1 copy.10
  406.7 73.6 %reduce-scatter.17.cloned.1.call-done = f32[48,256]{1,0:T(8,128)} async-done(((f32[768,256]{1,0:T(8,128)}), f32[48,256]{1,0:T(8,128)}) %reduce-scatter.17.cloned.1.call-update) | async-done | bytes 49168
  480.3 0.9 copy.16
  481.2 0.1 copy.9
  481.3 73.6 %reduce-scatter.13.cloned.1.call-done = f32[48,256]{1,0:T(8,128)} async-done(((f32[768,256]{1,0:T(8,128)}), f32[48,256]{1,0:T(8,128)}) %reduce-scatter.13.cloned.1.call-update) | async-done | bytes 49168
  554.9 0.9 copy.12
  555.8 0.1 copy.7
  555.9 73.7 %reduce-scatter.15.cloned.1.call-done = f32[48,256]{1,0:T(8,128)} async-done(((f32[768,256]{1,0:T(8,128)}), f32[48,256]{1,0:T(8,128)}) %reduce-scatter.15.cloned.1.call-update) | async-done | bytes 49168
  629.6 0.9 copy.14
  630.5 0.1 copy.8
  630.5 0.7 pad_maximum_fusion
  (12 shorter events, 0.2 us)
Async XLA Ops:
  6.5 11.7 %copy-start = (bf16[4,384,768]{2,1,0:T(8,128)(2,1)S(1)}, bf16[4,384,768]{2,1,0:T(8,128)(2,1)}, u32[]{:S(2)}) copy-start(bf16[4,384,768]{2,1,0:T(8,128)(2,1)} %param.5) | copy-start | bytes 7077892
  6.5 311.3 %all-reduce.3.cloned.1.call-start = ((), (), s32[]{:S(2)}) async-start(), calls=%async_computation.8 | async-start | bytes 6291456 | tf_op jit(solution)/shard_map/psum | solution.py:11
  24.9 380.8 %reduce-scatter.19.cloned.1.call-start = ((), (), s32[]{:S(2)}) async-start(), calls=%async_computation.7 | async-start | bytes 835584
  321.0 159.3 %reduce-scatter.17.cloned.1.call-start = ((), (), s32[]{:S(2)}) async-start(), calls=%async_computation.6 | async-start | bytes 835584
  324.1 230.8 %reduce-scatter.13.cloned.1.call-start = ((), (), s32[]{:S(2)}) async-start(), calls=%async_computation.4 | async-start | bytes 835584
  327.3 302.3 %reduce-scatter.15.cloned.1.call-start = ((), (), s32[]{:S(2)}) async-start(), calls=%async_computation.5 | async-start | bytes 835584
Sparse Core Ops, SparseCore 0:
  25.0 292.7 all-reduce.2
  321.1 84.6 reduce-scatter.18
  408.6 71.7 reduce-scatter.16
  483.2 71.6 reduce-scatter.12
  557.6 71.9 reduce-scatter.14
where the time goes:
time: 638 us
  waiting for transfers between devices  589 us (92%)
  between operations  18.4 us (3%)
  matrix products  14.3 us (2%)
  local copies, waits for them, and re-layouts  13.5 us (2%)
    unnamed x9, waiting for transfers between devices  296 us
    psum x1, waiting for transfers between devices, spread(): return lax.psum(block, axis)  293 us
  transfers between devices with their start and end apart: 5, of which 5 were waited for; matrix products, arithmetic and copies ran while one was open for 2% of the time, Pallas kernels for 0%

commit v1 on v0

v1 whole, which is shorter than its diff:
```python
import functools

import jax
import jax.numpy as jnp
from jax import lax
from jax.experimental import pallas as pl
from jax.experimental.pallas import tpu as pltpu
from jax.sharding import PartitionSpec as P

X = 4
ZH = 4
Y = 8
LANE = 128


def greet(peers):
    barrier = pltpu.get_barrier_semaphore()
    for axis, peer in peers:
        pl.semaphore_signal(
            barrier, inc=1, device_id={axis: peer}, device_id_type=pl.DeviceIdType.MESH
        )
    pl.semaphore_wait(barrier, len(peers))


def remote(src, dst, send, recv, axis, peer):
    copy = pltpu.make_async_remote_copy(
        src_ref=src,
        dst_ref=dst,
        send_sem=send,
        recv_sem=recv,
        device_id={axis: peer},
        device_id_type=pl.DeviceIdType.MESH,
    )
    copy.start()
    return copy


def share_kernel(
    mine, chosen, border, out, turned,
    pair_in, x_out, x_in, z_sum, z_in, z_out, full, home,
    pair_s, pair_r, xs, xr, zs, zr, zgs, zgr, xgs, xgr, bs, br, outs,
):
    at = lax.axis_index("col")
    core = lax.rem(at, 2)
    zh = lax.rem(lax.div(at, 2), ZH)
    x = lax.div(at, 2 * ZH)
    way = 1 - 2 * core
    other = 1 - core

    def col(xx, zz, cc):
        return (xx * ZH + zz) * 2 + cc

    xa, xb, xf = lax.rem(x + way + X, X), lax.rem(x - way + X, X), lax.rem(x + 2, X)
    za, zb, zf = lax.rem(zh + way + ZH, ZH), lax.rem(zh - way + ZH, ZH), lax.rem(zh + 2, ZH)
    partner = col(x, zh, other)
    x_fwd, x_back = col(xa, zh, core), col(xb, zh, core)
    z_fwd, z_back = col(x, za, core), col(x, zb, core)
    greet([("col", d) for d in (partner, x_fwd, x_back, z_fwd, z_back)])

    sends = []
    pair = {}
    for k, s in enumerate((xf, xa, xb, x)):
        pair[k] = remote(mine.at[other, s], pair_in.at[s], pair_s.at[k], pair_r.at[k], "col", partner)
    pair[0].wait_recv()
    x_out[0] = mine[core, xf] + pair_in[xf]
    c0 = remote(x_out.at[0], x_in.at[0], xs.at[0], xr.at[0], "col", x_fwd)
    pair[1].wait_recv()
    x_out[1] = mine[core, xb] + pair_in[xb]
    c1 = remote(x_out.at[1], x_in.at[1], xs.at[1], xr.at[1], "col", x_back)
    pair[2].wait_recv()
    x_out[2] = mine[core, xa] + pair_in[xa]
    scen, depth, rows = border.shape
    turned[:, 0:depth] = border[0].T
    c0.wait_recv()
    x_out[3] = x_out[2] + x_in[0]
    c2 = remote(x_out.at[3], x_in.at[2], xs.at[2], xr.at[2], "col", x_fwd)
    for s in range(1, scen):
        turned[:, s * depth:(s + 1) * depth] = border[s].T
    pair[3].wait_recv()
    c1.wait_recv()
    z_sum[...] = mine[core, x] + pair_in[x] + x_in[1]
    c2.wait_recv()
    z_sum[...] = z_sum[...] + x_in[2]

    d0 = remote(z_sum.at[zf], z_in.at[0], zs.at[0], zr.at[0], "col", z_fwd)
    d1 = remote(z_sum.at[zb], z_in.at[1], zs.at[1], zr.at[1], "col", z_back)
    d0.wait_recv()
    z_out[...] = z_sum[za] + z_in[0]
    d2 = remote(z_out, z_in.at[2], zs.at[2], zr.at[2], "col", z_fwd)
    d1.wait_recv()
    part = z_sum[zh] + z_in[1]
    d2.wait_recv()
    part = part + z_in[2]
    home[...] = jnp.dot(chosen[x], part, preferred_element_type=jnp.float32).astype(jnp.bfloat16)

    keep = pltpu.make_async_copy(home, full.at[core, x, zh], outs.at[0, 0])
    keep.start()
    e0 = remote(home, full.at[core, x, zh], zgs.at[0], zgr.at[0], "col", z_fwd)
    e1 = remote(home, full.at[core, x, zh], zgs.at[1], zgr.at[1], "col", z_back)
    e0.wait_recv()
    e2 = remote(full.at[core, x, zb], full.at[core, x, zb], zgs.at[2], zgr.at[2], "col", z_fwd)
    e1.wait_recv()
    keep.wait()
    e2.wait_recv()

    stores = []

    def store(cc, s, slot):
        for q in range(4):
            copy = pltpu.make_async_copy(
                full.at[cc, s, q],
                out.at[cc, q // 2, s, :, pl.ds((q % 2) * LANE, LANE)],
                outs.at[slot, q],
            )
            copy.start()
            stores.append(copy)

    def both(s, k):
        sends.append(
            remote(full.at[core, s], full.at[core, s], bs.at[k], br.at[k], "col", partner)
        )
        store(core, s, k)

    g0 = remote(full.at[core, x], full.at[core, x], xgs.at[0], xgr.at[0], "col", x_fwd)
    g1 = remote(full.at[core, x], full.at[core, x], xgs.at[1], xgr.at[1], "col", x_back)
    both(x, 0)
    g0.wait_recv()
    g2 = remote(full.at[core, xb], full.at[core, xb], xgs.at[2], xgr.at[2], "col", x_fwd)
    both(xb, 1)
    g1.wait_recv()
    both(xa, 2)
    sends[0].wait_recv()
    store(other, x, 4)
    sends[1].wait_recv()
    store(other, xa, 5)
    sends[2].wait_recv()
    store(other, xb, 6)
    g2.wait_recv()
    both(xf, 3)
    sends[3].wait_recv()
    store(other, xf, 7)
    for copy in [pair[k] for k in range(4)] + [c0, c1, c2, d0, d1, d2, e0, e1, e2, g0, g1, g2] + sends:
        copy.wait_send()
    for copy in stores:
        copy.wait()


def share(mine, chosen, border):
    _, xn, zn, depth, lane = mine.shape
    scen, _, rows = border.shape
    piece = (depth, lane)
    chunk = (zn,) + piece
    bf = jnp.bfloat16
    dma = pltpu.SemaphoreType.DMA
    vm = pl.BlockSpec(memory_space=pltpu.VMEM)
    return pl.pallas_call(
        share_kernel,
        out_shape=(
            jax.ShapeDtypeStruct((2, 2, scen, depth, 2 * lane), bf),
            jax.ShapeDtypeStruct((rows, scen * depth), bf),
        ),
        in_specs=[vm, vm, vm],
        out_specs=(pl.BlockSpec(memory_space=pl.ANY), vm),
        scratch_shapes=[
            pltpu.VMEM((xn,) + chunk, bf),
            pltpu.VMEM((4,) + chunk, bf),
            pltpu.VMEM((3,) + chunk, bf),
            pltpu.VMEM(chunk, bf),
            pltpu.VMEM((3,) + piece, bf),
            pltpu.VMEM(piece, bf),
            pltpu.VMEM((2, xn) + chunk, bf),
            pltpu.VMEM(piece, bf),
            dma((4,)), dma((4,)),
            dma((3,)), dma((3,)),
            dma((3,)), dma((3,)),
            dma((3,)), dma((3,)),
            dma((3,)), dma((3,)),
            dma((4,)), dma((4,)),
            dma((8, 4)),
        ],
        compiler_params=pltpu.CompilerParams(
            collective_id=0, has_side_effects=True, vmem_limit_bytes=48 * 1024 * 1024
        ),
    )(mine, chosen, border)


def reduce_kernel(
    turned, shared, out,
    own, a_out, a_in, b_out, b_in, half_out, half_in,
    a_s, a_r, b_s, b_r, h_s, h_r,
):
    at = lax.axis_index("grp")
    zl = lax.rem(at, 2)
    y = lax.div(at, 2)
    core = lax.rem(lax.axis_index("col"), 2)
    way = 1 - 2 * core

    def ring(step):
        return lax.rem(y + step * way + 2 * Y, Y)

    fwd, back = ring(1) * 2 + zl, ring(-1) * 2 + zl
    mate = y * 2 + (1 - zl)
    greet([("grp", d) for d in (fwd, back, mate)])

    panels = shared.shape[0]
    far, near = Y // 2, Y // 2 - 1
    sent = []
    ahead, behind, halves = {}, {}, {}

    def product(p):
        whole = jnp.dot(turned[...], shared[p], preferred_element_type=jnp.float32)
        own[p] = whole.reshape(own.shape[1:])

    def hop(p, t):
        term = own[p, ring(far - t)]
        if t > 0:
            ahead[p].wait_recv()
            term = term + a_in[p, t - 1].astype(jnp.float32)
        a_out[p, t] = term.astype(jnp.bfloat16)
        ahead[p] = remote(a_out.at[p, t], a_in.at[p, t], a_s.at[p, t], a_r.at[p, t], "grp", fwd)
        sent.append(ahead[p])
        if t < near:
            term = own[p, ring(t - near)]
            if t > 0:
                behind[p].wait_recv()
                term = term + b_in[p, t - 1].astype(jnp.float32)
            b_out[p, t] = term.astype(jnp.bfloat16)
            behind[p] = remote(b_out.at[p, t], b_in.at[p, t], b_s.at[p, t], b_r.at[p, t], "grp", back)
            sent.append(behind[p])

    def meet(p):
        behind[p].wait_recv()
        ahead[p].wait_recv()

        def total(z):
            return (
                own[p, y, z]
                + a_in[p, far - 1, z].astype(jnp.float32)
                + b_in[p, near - 1, z].astype(jnp.float32)
            )

        half_out[p] = total(1 - zl)
        halves[p] = remote(half_out.at[p], half_in.at[p], h_s.at[p], h_r.at[p], "grp", mate)
        sent.append(halves[p])
        out[p] = total(zl)

    def finish(p):
        halves[p].wait_recv()
        out[p] = out[p] + half_in[p]

    for u in range(panels + far + 1):
        if u < panels:
            product(u)
        for p in range(panels):
            t = u - p
            if 0 <= t < far:
                hop(p, t)
            elif t == far:
                meet(p)
            elif t == far + 1:
                finish(p)
    for copy in sent:
        copy.wait_send()


def reduce_over_groups(turned, shared):
    panels, _, width = shared.shape
    rows = turned.shape[0] // (2 * Y)
    block = (2, rows, width)
    far, near = Y // 2, Y // 2 - 1
    f32, bf = jnp.float32, jnp.bfloat16
    dma = pltpu.SemaphoreType.DMA
    vm = pl.BlockSpec(memory_space=pltpu.VMEM)
    return pl.pallas_call(
        reduce_kernel,
        out_shape=jax.ShapeDtypeStruct((panels, rows, width), f32),
        in_specs=[vm, vm],
        out_specs=vm,
        scratch_shapes=[
            pltpu.VMEM((panels, Y) + block, f32),
            pltpu.VMEM((panels, far) + block, bf),
            pltpu.VMEM((panels, far) + block, bf),
            pltpu.VMEM((panels, near) + block, bf),
            pltpu.VMEM((panels, near) + block, bf),
            pltpu.VMEM((panels, rows, width), f32),
            pltpu.VMEM((panels, rows, width), f32),
            dma((panels, far)), dma((panels, far)),
            dma((panels, near)), dma((panels, near)),
            dma((panels,)), dma((panels,)),
        ],
        compiler_params=pltpu.CompilerParams(
            collective_id=1, has_side_effects=True, vmem_limit_bytes=48 * 1024 * 1024
        ),
    )(turned, shared)


def on_device(border, inverses, scen_map, owners, slots):
    scen, depth, _ = border.shape
    width = 2 * LANE
    chosen = jnp.take(inverses, scen_map[0], axis=0)
    me = lax.axis_index("col")
    panels = []
    for p in range(owners.shape[0]):
        panel = lax.dynamic_slice_in_dim(border, slots[p] * width, width, 2)
        panels.append(jnp.where(owners[p] == me, panel, jnp.zeros_like(panel)))
    mine = jnp.stack(panels).reshape(2, 2, scen, depth, 2, LANE)
    mine = mine.transpose(0, 2, 1, 4, 3, 5).reshape(2, scen, 4, depth, LANE)
    shared, turned = share(mine, chosen, border)
    shared = shared.reshape(4, scen * depth, width)
    return reduce_over_groups(turned, shared)


def solution(mesh):
    return jax.shard_map(
        on_device,
        mesh=mesh,
        in_specs=(P("grp", None, "col"), P("grp", None, None), P("grp", None), P(), P()),
        out_specs=P(None, ("col", "grp"), None),
        check_vma=False,
    )
```

time: 638 us -> 137 us (0.21)
  the two profiles are of different devices: /device:TPU:6 before, /device:TPU:8 now
where the time goes in v1:
time: 137 us; the launch traced here: 136 us
  Pallas kernels  107 us (78%)
  local copies, waits for them, and re-layouts  17.1 us (12%)
  other arithmetic  6.51 us (5%)
  between operations  5.12 us (4%)
    pallas_call x1, Pallas kernels, share(): pl.pallas_call(share_kernel, out_shape=(jax.ShapeDtypeStruct((2, 2, scen,...  69.3 us
    pallas_call x1, Pallas kernels, reduce_over_groups(): pl.pallas_call(reduce_kernel, out_shape=jax.ShapeDtypeStruct((panels, row...  37.9 us
    reshape x2, local copies, waits for them, and re-layouts, on_device(): mine = jnp.stack(panels).reshape(2, 2, scen, depth, 2, LANE)  9.88 us
    select_n x2, other arithmetic, on_device(): chosen = jnp.take(inverses, scen_map[0], axis=0)  3.28 us

profile of v1, /device:TPU:8, one launch (start us, length us, event | category | flops | bytes accessed | tf_op | source)
XLA Modules:
  0.0 136.1 jit_solution(6318845179307382785)
XLA Ops:
  0.0 0.0 copy-start
  0.0 0.8 fusion
  0.8 0.7 compare_and_fusion
  1.4 1.5 %fusion.1 = (s32[1]{0:T(128)}, s32[1]{0:T(128)}, s32[1]{0:T(128)}, s32[1]{0:T(128)}) fusion(s32[4]{0:T(128)} %param.8), kind=kLoop, calls=%fused_computation.12 | loop fusion | bytes 32 | tf_op jit(solution)/shard_map/slice | solution.py:305
  5.4 1.5 %fusion.2 = (s32[1]{0:T(128)}, s32[1]{0:T(128)}, s32[1]{0:T(128)}, s32[1]{0:T(128)}) fusion(s32[4]{0:T(128)} %param.9), kind=kLoop, calls=%fused_computation.13 | loop fusion | bytes 32 | tf_op jit(solution)/shard_map/slice | solution.py:304
  9.4 0.0 copy-done
  9.4 0.0 copy-start.1
  9.4 1.8 %gather_fusion = bf16[4,384,384]{2,1,0:T(8,128)(2,1)} fusion(bf16[4,384,384]{2,1,0:T(8,128)(2,1)S(1)} %copy-done, s32[1024]{0:T(1024)S(1)} %pad_clamp_fusion), kind=kCustom, calls=%fused_computation | custom fusion | bytes 2359312 | tf_op jit(solution)/shard_map/jit(_take)/gather | solution.py:300
  11.2 2.5 %broadcast_select_fusion.chosen = bf16[4,384,384]{2,1,0:T(8,128)(2,1)} fusion(bf16[4,384,384]{2,1,0:T(8,128)(2,1)} %gather_fusion, pred[4]{0:T(512)(128)(4,1)S(1)} %compare_and_fusion), kind=kLoop, calls=%fused_computation.2 | loop fusion | flops 589824 | bytes 2359300 | tf_op jit(solution)/shard_map/jit(_take)/select_n | solution.py:300
  13.7 0.0 copy-done.1
  13.7 0.7 select_bitcast_fusion.3
  14.4 1.9 %pad_maximum_fusion = bf16[4,4,384,256]{3,2,1,0:T(8,128)(2,1)} fusion(bf16[1,4,384,256]{3,2,1,0:T(8,128)(2,1)S(1)} %get-tuple-element.12, bf16[1,4,384,256]{3,2,1,0:T(8,128)(2,1)S(1)} %get-tuple-element.10, bf16[1,4,384,256]{3,2,1,0:T(8,128)(2,1)S(1)} %get-tuple-element.11, bf16[1,4,384,256]{3,2,1,0:T(8,128)(2,1)S(1)} %get-tuple-element.9), kind=kLoop, calls=%fused_computation.1 | loop fusion | flops 4718592 | bytes 6291456 | tf_op jit(solution)/shard_map/stack | solution.py:306
  16.3 5.5 %reshape.51 = bf16[2,2,4,384,2,128]{5,4,3,2,1,0:T(2,128)(2,1)} reshape(bf16[4,4,384,256]{3,2,1,0:T(8,128)(2,1)} %pad_maximum_fusion) | data formatting | bytes 6291456 | tf_op jit(solution)/shard_map/reshape | solution.py:306
  21.8 0.0 copy-start.2
  21.8 4.4 %copy.6 = bf16[2,2,4,384,2,128]{5,3,4,1,2,0:T(8,128)(2,1)} copy(bf16[2,2,4,384,2,128]{5,4,3,2,1,0:T(2,128)(2,1)} %reshape.51) | data formatting | bytes 6291456 | tf_op jit(solution)/shard_map/reshape | solution.py:306
  26.2 0.0 copy-done.2
  26.2 69.3 %shard_map.55 = (bf16[2,2,4,384,256]{4,3,2,1,0:T(8,128)(2,1)}, bf16[768,1536]{1,0:T(8,128)(2,1)S(1)}) custom-call(bf16[2,4,4,384,128]{4,3,2,1,0:T(8,128)(2,1)} %bitcast.29, bf16[4,384,384]{2,1,0:T(8,128)(2,1)S(1)} %copy-done.2, bf16[4,384,768]{2,1,0:T(8,128)(2,1)S(1)} %copy-done.1), custom_call_target="tpu_custom_call" | custom-call | tf_op jit(solution)/shard_map/pallas_call | solution.py:156
  95.5 0.0 copy-start.3
  95.6 1.9 %copy-done.3 = bf16[2,2,4,384,256]{4,3,2,1,0:T(8,128)(2,1)S(1)} copy-done((bf16[2,2,4,384,256]{4,3,2,1,0:T(8,128)(2,1)S(1)}, bf16[2,2,4,384,256]{4,3,2,1,0:T(8,128)(2,1)}, u32[]{:S(2)}) %copy-start.3) | copy-done | bytes 3145752
  97.4 37.9 %shard_map.56 = f32[4,48,256]{2,1,0:T(8,128)S(1)} custom-call(bf16[768,1536]{1,0:T(8,128)(2,1)S(1)} %get-tuple-element.7.turned, bf16[4,1536,256]{2,1,0:T(8,128)(2,1)S(1)} %bitcast.28), custom_call_target="tpu_custom_call" | custom-call | tf_op jit(solution)/shard_map/pallas_call | solution.py:274
  135.4 0.7 copy.8
  (1 shorter events, 0.0 us)
Async XLA Ops:
  0.0 9.4 %copy-start = (bf16[4,384,384]{2,1,0:T(8,128)(2,1)S(1)}, bf16[4,384,384]{2,1,0:T(8,128)(2,1)}, u32[]{:S(2)}) copy-start(bf16[4,384,384]{2,1,0:T(8,128)(2,1)} %param.6) | copy-start | bytes 3538948
  9.4 4.3 %copy-start.1 = (bf16[4,384,768]{2,1,0:T(8,128)(2,1)S(1)}, bf16[4,384,768]{2,1,0:T(8,128)(2,1)}, u32[]{:S(2)}) copy-start(bf16[4,384,768]{2,1,0:T(8,128)(2,1)} %border.1) | copy-start | bytes 7077892
  21.8 4.4 %copy-start.2 = (bf16[4,384,384]{2,1,0:T(8,128)(2,1)S(1)}, bf16[4,384,384]{2,1,0:T(8,128)(2,1)}, u32[]{:S(2)}) copy-start(bf16[4,384,384]{2,1,0:T(8,128)(2,1)} %broadcast_select_fusion.chosen) | copy-start | bytes 3538948
  95.5 1.9 %copy-start.3 = (bf16[2,2,4,384,256]{4,3,2,1,0:T(8,128)(2,1)S(1)}, bf16[2,2,4,384,256]{4,3,2,1,0:T(8,128)(2,1)}, u32[]{:S(2)}) copy-start(bf16[2,2,4,384,256]{4,3,2,1,0:T(8,128)(2,1)} %get-tuple-element.8) | copy-start | bytes 9437188

commit v2 on v1

--- a/solution.py
+++ b/solution.py
@@ -11,6 +11,7 @@
 ZH = 4
 Y = 8
 LANE = 128
+TILE = 16
 
 
 def greet(peers):
@@ -36,8 +37,8 @@
 
 
 def share_kernel(
-    mine, chosen, border, out, turned,
-    pair_in, x_out, x_in, z_sum, z_in, z_out, full, home,
+    owners, slots, scen_map, border, inverses, out, turned,
+    marks, picked, pair_out, pair_in, x_out, x_in, z_sum, z_in, z_out, full, home,
     pair_s, pair_r, xs, xr, zs, zr, zgs, zgr, xgs, xgr, bs, br, outs,
 ):
     at = lax.axis_index("col")
@@ -50,6 +51,24 @@
     def col(xx, zz, cc):
         return (xx * ZH + zz) * 2 + cc
 
+    def flag(left, right):
+        same = jnp.full((TILE, LANE), left, jnp.int32) == jnp.full((TILE, LANE), right, jnp.int32)
+        return jnp.where(same, 1.0, 0.0)
+
+    tiles = border.shape[1] // TILE
+    for p in range(owners.shape[0]):
+        for k in range(3):
+            marks[p, k] = (flag(owners[p], at) * flag(slots[p], k)).astype(jnp.bfloat16)
+
+    def panel(cc, s, q):
+        total = None
+        for k in range(3):
+            start = k * 2 * LANE + (q % 2) * LANE
+            block = border[s, :, start:start + LANE].reshape(tiles, TILE, LANE)
+            term = block * marks[2 * cc + q // 2, k][None]
+            total = term if total is None else total + term
+        return total.reshape(tiles * TILE, LANE)
+
     xa, xb, xf = lax.rem(x + way + X, X), lax.rem(x - way + X, X), lax.rem(x + 2, X)
     za, zb, zf = lax.rem(zh + way + ZH, ZH), lax.rem(zh - way + ZH, ZH), lax.rem(zh + 2, ZH)
     partner = col(x, zh, other)
@@ -60,17 +79,29 @@
     sends = []
     pair = {}
     for k, s in enumerate((xf, xa, xb, x)):
-        pair[k] = remote(mine.at[other, s], pair_in.at[s], pair_s.at[k], pair_r.at[k], "col", partner)
+        for q in range(4):
+            pair_out[k, q] = panel(other, s, q)
+        pair[k] = remote(pair_out.at[k], pair_in.at[s], pair_s.at[k], pair_r.at[k], "col", partner)
     pair[0].wait_recv()
-    x_out[0] = mine[core, xf] + pair_in[xf]
+    for q in range(4):
+        x_out[0, q] = panel(core, xf, q) + pair_in[xf, q]
     c0 = remote(x_out.at[0], x_in.at[0], xs.at[0], xr.at[0], "col", x_fwd)
     pair[1].wait_recv()
-    x_out[1] = mine[core, xb] + pair_in[xb]
+    for q in range(4):
+        x_out[1, q] = panel(core, xb, q) + pair_in[xb, q]
     c1 = remote(x_out.at[1], x_in.at[1], xs.at[1], xr.at[1], "col", x_back)
     pair[2].wait_recv()
-    x_out[2] = mine[core, xa] + pair_in[xa]
+    for q in range(4):
+        x_out[2, q] = panel(core, xa, q) + pair_in[xa, q]
     scen, depth, rows = border.shape
     turned[:, 0:depth] = border[0].T
+    for lane in range(0, depth, LANE):
+        total = None
+        for k in range(scen):
+            mark = flag(scen_map[0, x], k).astype(jnp.bfloat16)
+            term = inverses[k, :, lane:lane + LANE].reshape(tiles, TILE, LANE) * mark[None]
+            total = term if total is None else total + term
+        picked[:, lane:lane + LANE] = total.reshape(depth, LANE)
     c0.wait_recv()
     x_out[3] = x_out[2] + x_in[0]
     c2 = remote(x_out.at[3], x_in.at[2], xs.at[2], xr.at[2], "col", x_fwd)
@@ -78,7 +109,8 @@
         turned[:, s * depth:(s + 1) * depth] = border[s].T
     pair[3].wait_recv()
     c1.wait_recv()
-    z_sum[...] = mine[core, x] + pair_in[x] + x_in[1]
+    for q in range(4):
+        z_sum[q] = panel(core, x, q) + pair_in[x, q] + x_in[1, q]
     c2.wait_recv()
     z_sum[...] = z_sum[...] + x_in[2]
 
@@ -91,7 +123,7 @@
     part = z_sum[zh] + z_in[1]
     d2.wait_recv()
     part = part + z_in[2]
-    home[...] = jnp.dot(chosen[x], part, preferred_element_type=jnp.float32).astype(jnp.bfloat16)
+    home[...] = jnp.dot(picked[...], part, preferred_element_type=jnp.float32).astype(jnp.bfloat16)
 
     keep = pltpu.make_async_copy(home, full.at[core, x, zh], outs.at[0, 0])
     keep.start()
@@ -145,23 +177,27 @@
         copy.wait()
 
 
-def share(mine, chosen, border):
-    _, xn, zn, depth, lane = mine.shape
-    scen, _, rows = border.shape
+def share(owners, slots, scen_map, border, inverses):
+    scen, depth, rows = border.shape
+    lane, xn = LANE, X
     piece = (depth, lane)
-    chunk = (zn,) + piece
+    chunk = (ZH,) + piece
     bf = jnp.bfloat16
     dma = pltpu.SemaphoreType.DMA
     vm = pl.BlockSpec(memory_space=pltpu.VMEM)
+    sm = pl.BlockSpec(memory_space=pltpu.SMEM)
     return pl.pallas_call(
         share_kernel,
         out_shape=(
             jax.ShapeDtypeStruct((2, 2, scen, depth, 2 * lane), bf),
             jax.ShapeDtypeStruct((rows, scen * depth), bf),
         ),
-        in_specs=[vm, vm, vm],
-        out_specs=(pl.BlockSpec(memory_space=pl.ANY), vm),
+        in_specs=[sm, sm, sm, vm, vm],
+        out_specs=(vm, vm),
         scratch_shapes=[
+            pltpu.VMEM((4, 3, TILE, LANE), bf),
+            pltpu.VMEM((depth, depth), bf),
+            pltpu.VMEM((xn,) + chunk, bf),
             pltpu.VMEM((xn,) + chunk, bf),
             pltpu.VMEM((4,) + chunk, bf),
             pltpu.VMEM((3,) + chunk, bf),
@@ -179,9 +215,9 @@
             dma((8, 4)),
         ],
         compiler_params=pltpu.CompilerParams(
-            collective_id=0, has_side_effects=True, vmem_limit_bytes=48 * 1024 * 1024
+            collective_id=0, has_side_effects=True, vmem_limit_bytes=24 * 1024 * 1024
         ),
-    )(mine, chosen, border)
+    )(owners, slots, scen_map, border, inverses)
 
 
 def reduce_kernel(
@@ -200,9 +236,9 @@
 
     fwd, back = ring(1) * 2 + zl, ring(-1) * 2 + zl
     mate = y * 2 + (1 - zl)
+    panels = shared.shape[0]
     greet([("grp", d) for d in (fwd, back, mate)])
 
-    panels = shared.shape[0]
     far, near = Y // 2, Y // 2 - 1
     sent = []
     ahead, behind, halves = {}, {}, {}
@@ -289,24 +325,15 @@
             dma((panels,)), dma((panels,)),
         ],
         compiler_params=pltpu.CompilerParams(
-            collective_id=1, has_side_effects=True, vmem_limit_bytes=48 * 1024 * 1024
+            collective_id=1, has_side_effects=True, vmem_limit_bytes=24 * 1024 * 1024
         ),
     )(turned, shared)
 
 
 def on_device(border, inverses, scen_map, owners, slots):
     scen, depth, _ = border.shape
-    width = 2 * LANE
-    chosen = jnp.take(inverses, scen_map[0], axis=0)
-    me = lax.axis_index("col")
-    panels = []
-    for p in range(owners.shape[0]):
-        panel = lax.dynamic_slice_in_dim(border, slots[p] * width, width, 2)
-        panels.append(jnp.where(owners[p] == me, panel, jnp.zeros_like(panel)))
-    mine = jnp.stack(panels).reshape(2, 2, scen, depth, 2, LANE)
-    mine = mine.transpose(0, 2, 1, 4, 3, 5).reshape(2, scen, 4, depth, LANE)
-    shared, turned = share(mine, chosen, border)
-    shared = shared.reshape(4, scen * depth, width)
+    shared, turned = share(owners, slots, scen_map, border, inverses)
+    shared = shared.reshape(4, scen * depth, 2 * LANE)
     return reduce_over_groups(turned, shared)
 
 

time: 137 us -> 111 us (0.81)
  the two profiles are of different devices: /device:TPU:8 before, /device:TPU:6 now
where the time goes in v2:
time: 111 us; the launch traced here: 110 us
  Pallas kernels  104 us (94%)
  local copies, waits for them, and re-layouts  5.58 us (5%)
    pallas_call x1, Pallas kernels, share(): pl.pallas_call(share_kernel, out_shape=(jax.ShapeDtypeStruct((2, 2, scen,...  64.4 us
    pallas_call x1, Pallas kernels, reduce_over_groups(): pl.pallas_call(reduce_kernel, out_shape=jax.ShapeDtypeStruct((panels, row...  39.8 us
    unnamed x11, local copies, waits for them, and re-layouts  5.58 us

profile of v2, /device:TPU:6, one launch (start us, length us, event | category | flops | bytes accessed | tf_op | source)
XLA Modules:
  0.0 109.8 jit_solution(3270371113668210571)
XLA Ops:
  0.0 0.0 copy-start
  0.0 1.7 %copy-done = bf16[4,384,768]{2,1,0:T(8,128)(2,1)S(1)} copy-done((bf16[4,384,768]{2,1,0:T(8,128)(2,1)S(1)}, bf16[4,384,768]{2,1,0:T(8,128)(2,1)}, u32[]{:S(2)}) %copy-start) | copy-done | bytes 2359320
  1.7 0.0 copy-start.1
  1.7 1.3 %copy-done.1 = bf16[4,384,384]{2,1,0:T(8,128)(2,1)S(1)} copy-done((bf16[4,384,384]{2,1,0:T(8,128)(2,1)S(1)}, bf16[4,384,384]{2,1,0:T(8,128)(2,1)}, u32[]{:S(2)}) %copy-start.1) | copy-done | bytes 1179672
  2.9 0.0 copy-start.2
  2.9 0.7 copy-done.2
  3.6 0.0 copy-start.3
  3.6 0.7 copy-done.3
  4.2 0.0 copy-start.4
  4.3 0.7 copy-done.4
  4.9 64.4 %shard_map.55 = (bf16[2,2,4,384,256]{4,3,2,1,0:T(8,128)(2,1)S(1)}, bf16[768,1536]{1,0:T(8,128)(2,1)S(1)}) custom-call(s32[4]{0:T(128)S(1)} %copy-done.2, s32[4]{0:T(128)S(1)} %copy-done.3, s32[1,4]{1,0:T(1,128)S(1)} %copy-done.4, bf16[4,384,768]{2,1,0:T(8,128)(2,1)S(1)} %copy-done, bf16[4,384,384]{2,1,0:T(8,128)(2,1)S(1)} %copy-done.1), custom_call_target="tpu_custom_call" | custom-call | tf_op jit(solution)/shard_map/pallas_call | solution.py:189
  69.3 39.8 %shard_map.56 = f32[4,48,256]{2,1,0:T(8,128)S(1)} custom-call(bf16[768,1536]{1,0:T(8,128)(2,1)S(1)} %get-tuple-element.7.turned, bf16[4,1536,256]{2,1,0:T(8,128)(2,1)S(1)} %bitcast.1), custom_call_target="tpu_custom_call" | custom-call | tf_op jit(solution)/shard_map/pallas_call | solution.py:310
  109.1 0.7 copy.7
Async XLA Ops:
  0.0 1.7 %copy-start = (bf16[4,384,768]{2,1,0:T(8,128)(2,1)S(1)}, bf16[4,384,768]{2,1,0:T(8,128)(2,1)}, u32[]{:S(2)}) copy-start(bf16[4,384,768]{2,1,0:T(8,128)(2,1)} %border.1) | copy-start | bytes 7077892
  1.7 1.3 %copy-start.1 = (bf16[4,384,384]{2,1,0:T(8,128)(2,1)S(1)}, bf16[4,384,384]{2,1,0:T(8,128)(2,1)}, u32[]{:S(2)}) copy-start(bf16[4,384,384]{2,1,0:T(8,128)(2,1)} %inverses.1) | copy-start | bytes 3538948
  2.9 0.7 copy-start.2
  3.6 0.7 copy-start.3
  4.2 0.7 copy-start.4

commit v3 on v2

v3 whole, which is shorter than its diff:
```python
import functools

import jax
import jax.numpy as jnp
from jax import lax
from jax.experimental import pallas as pl
from jax.experimental.pallas import tpu as pltpu
from jax.sharding import PartitionSpec as P

X = 4
ZH = 4
Y = 8
LANE = 128
TILE = 16


def greet(peers):
    barrier = pltpu.get_barrier_semaphore()
    for axis, peer in peers:
        pl.semaphore_signal(
            barrier, inc=1, device_id={axis: peer}, device_id_type=pl.DeviceIdType.MESH
        )
    pl.semaphore_wait(barrier, len(peers))


def remote(src, dst, send, recv, axis, peer):
    copy = pltpu.make_async_remote_copy(
        src_ref=src,
        dst_ref=dst,
        send_sem=send,
        recv_sem=recv,
        device_id={axis: peer},
        device_id_type=pl.DeviceIdType.MESH,
    )
    copy.start()
    return copy


def share_kernel(
    owners, slots, scen_map, border, inverses, full, turned,
    marks, picked, pair_out, pair_in, x_out, x_own, x_in, z_sum, z_in, z_out, home,
    pair_s, pair_r, xs, xr, zs, zr, zgs, zgr, xgs, xgr, bs, br,
):
    at = lax.axis_index("col")
    core = lax.rem(at, 2)
    zh = lax.rem(lax.div(at, 2), ZH)
    x = lax.div(at, 2 * ZH)
    way = 1 - 2 * core
    other = 1 - core

    def col(xx, zz, cc):
        return (xx * ZH + zz) * 2 + cc

    def flag(left, right):
        same = jnp.full((TILE, LANE), left, jnp.int32) == jnp.full((TILE, LANE), right, jnp.int32)
        return jnp.where(same, 1.0, 0.0)

    scen, depth, _ = border.shape
    parts = depth // LANE
    tiles = LANE // TILE
    for p in range(owners.shape[0]):
        for k in range(3):
            marks[p, k] = (flag(owners[p], at) * flag(slots[p], k)).astype(jnp.bfloat16)

    def panel(cc, s, r, q):
        total = None
        for k in range(3):
            start = k * 2 * LANE + (q % 2) * LANE
            block = border[s, r * LANE:(r + 1) * LANE, start:start + LANE]
            block = block.reshape(tiles, TILE, LANE)
            term = block * marks[2 * cc + q // 2, k][None]
            total = term if total is None else total + term
        return total.reshape(LANE, LANE)

    def turn(s):
        turned[:, s * depth:(s + 1) * depth] = border[s].T

    xa, xb, xf = lax.rem(x + way + X, X), lax.rem(x - way + X, X), lax.rem(x + 2, X)
    za, zb, zf = lax.rem(zh + way + ZH, ZH), lax.rem(zh - way + ZH, ZH), lax.rem(zh + 2, ZH)
    partner = col(x, zh, other)
    x_fwd, x_back = col(xa, zh, core), col(xb, zh, core)
    z_fwd, z_back = col(x, za, core), col(x, zb, core)
    greet([("col", d) for d in (partner, x_fwd, x_back, z_fwd, z_back)])

    order = range(parts)
    sends = []

    def send(*args):
        copy = remote(*args)
        sends.append(copy)
        return copy

    pair = {}
    for k, s in enumerate((xf, xa, xb, x)):
        for r in order:
            for q in range(ZH):
                pair_out[k, r, q] = panel(other, s, r, q)
            pair[k, r] = send(
                pair_out.at[k, r], pair_in.at[s, r], pair_s.at[k, r], pair_r.at[k, r], "col", partner
            )

    def joined(k, s, r, q):
        return panel(core, s, r, q) + pair_in[s, r, q]

    c = {}
    for k, s, peer in ((0, xf, x_fwd), (1, xb, x_back)):
        for r in order:
            pair[k, r].wait_recv()
            for q in range(ZH):
                x_out[k, r, q] = joined(k, s, r, q)
            c[k, r] = send(x_out.at[k, r], x_in.at[k, r], xs.at[k, r], xr.at[k, r], "col", peer)
    for r in order:
        pair[2, r].wait_recv()
        for q in range(ZH):
            x_own[0, r, q] = joined(2, xa, r, q)
    turn(0)
    for r in order:
        c[0, r].wait_recv()
        for q in range(ZH):
            x_out[2, r, q] = x_own[0, r, q] + x_in[0, r, q]
        c[2, r] = send(x_out.at[2, r], x_in.at[2, r], xs.at[2, r], xr.at[2, r], "col", x_fwd)
    for lane in range(0, depth, LANE):
        for r in order:
            total = None
            for k in range(scen):
                mark = flag(scen_map[0, x], k).astype(jnp.bfloat16)
                block = inverses[k, r * LANE:(r + 1) * LANE, lane:lane + LANE]
                term = block.reshape(tiles, TILE, LANE) * mark[None]
                total = term if total is None else total + term
            picked[r * LANE:(r + 1) * LANE, lane:lane + LANE] = total.reshape(LANE, LANE)
    for r in order:
        pair[3, r].wait_recv()
        c[1, r].wait_recv()
        for q in range(ZH):
            x_own[1, r, q] = joined(3, x, r, q) + x_in[1, r, q]
    turn(1)

    d = {}

    def relay(r):
        d[0, r].wait_recv()
        z_out[r] = z_sum[r, za] + z_in[0, r]
        d[2, r] = send(z_out.at[r], z_in.at[2, r], zs.at[2, r], zr.at[2, r], "col", z_fwd)

    for r in order:
        c[2, r].wait_recv()
        for q in range(ZH):
            z_sum[r, q] = x_own[1, r, q] + x_in[2, r, q]
        d[0, r] = send(z_sum.at[r, zf], z_in.at[0, r], zs.at[0, r], zr.at[0, r], "col", z_fwd)
        d[1, r] = send(z_sum.at[r, zb], z_in.at[1, r], zs.at[1, r], zr.at[1, r], "col", z_back)
        if r > 0:
            relay(r - 1)
    relay(parts - 1)
    result = None
    for r in order:
        d[1, r].wait_recv()
        part = z_sum[r, zh] + z_in[1, r]
        d[2, r].wait_recv()
        part = part + z_in[2, r]
        term = jnp.dot(
            picked[:, r * LANE:(r + 1) * LANE], part, preferred_element_type=jnp.float32
        )
        result = term if result is None else result + term

    e = {}
    for r in order:
        home[r] = result[r * LANE:(r + 1) * LANE].astype(jnp.bfloat16)
        for k, peer in ((0, z_fwd), (1, z_back)):
            e[k, r] = send(
                home.at[r], full.at[core, x, r, zh], zgs.at[k, r], zgr.at[k, r], "col", peer
            )
        full[core, x, r, zh] = home[r]

    def pass_on(k, s, r, sent, got, axis, peer):
        return send(full.at[core, s, r], full.at[core, s, r], sent.at[k, r], got.at[k, r], axis, peer)

    for r in order:
        e[0, r].wait_recv()
        held = full.at[core, x, r, zb]
        e[2, r] = send(held, held, zgs.at[2, r], zgr.at[2, r], "col", z_fwd)
    g, h = {}, {}
    for r in order:
        e[1, r].wait_recv()
        e[2, r].wait_recv()
        g[0, r] = pass_on(0, x, r, xgs, xgr, "col", x_fwd)
        g[1, r] = pass_on(1, x, r, xgs, xgr, "col", x_back)
        h[0, r] = pass_on(0, x, r, bs, br, "col", partner)
    turn(2)
    for r in order:
        g[0, r].wait_recv()
        g[2, r] = pass_on(2, xb, r, xgs, xgr, "col", x_fwd)
        h[1, r] = pass_on(1, xb, r, bs, br, "col", partner)
    turn(3)
    for r in order:
        g[1, r].wait_recv()
        h[2, r] = pass_on(2, xa, r, bs, br, "col", partner)
    for r in order:
        g[2, r].wait_recv()
        h[3, r] = pass_on(3, xf, r, bs, br, "col", partner)
    for copy in h.values():
        copy.wait_recv()
    for copy in sends:
        copy.wait_send()


def share(owners, slots, scen_map, border, inverses):
    scen, depth, rows = border.shape
    parts = depth // LANE
    piece = (parts, LANE, LANE)
    chunk = (parts, ZH, LANE, LANE)
    bf = jnp.bfloat16
    dma = pltpu.SemaphoreType.DMA
    vm = pl.BlockSpec(memory_space=pltpu.VMEM)
    sm = pl.BlockSpec(memory_space=pltpu.SMEM)
    return pl.pallas_call(
        share_kernel,
        out_shape=(
            jax.ShapeDtypeStruct((2, X) + chunk, bf),
            jax.ShapeDtypeStruct((rows, scen * depth), bf),
        ),
        in_specs=[sm, sm, sm, vm, vm],
        out_specs=(vm, vm),
        scratch_shapes=[
            pltpu.VMEM((4, 3, TILE, LANE), bf),
            pltpu.VMEM((depth, depth), bf),
            pltpu.VMEM((X,) + chunk, bf),
            pltpu.VMEM((X,) + chunk, bf),
            pltpu.VMEM((3,) + chunk, bf),
            pltpu.VMEM((2,) + chunk, bf),
            pltpu.VMEM((3,) + chunk, bf),
            pltpu.VMEM(chunk, bf),
            pltpu.VMEM((3,) + piece, bf),
            pltpu.VMEM(piece, bf),
            pltpu.VMEM(piece, bf),
            dma((4, parts)), dma((4, parts)),
            dma((3, parts)), dma((3, parts)),
            dma((3, parts)), dma((3, parts)),
            dma((3, parts)), dma((3, parts)),
            dma((3, parts)), dma((3, parts)),
            dma((4, parts)), dma((4, parts)),
        ],
        compiler_params=pltpu.CompilerParams(
            collective_id=0, has_side_effects=True, vmem_limit_bytes=24 * 1024 * 1024
        ),
    )(owners, slots, scen_map, border, inverses)


def reduce_kernel(
    turned, shared, out,
    own, a_out, a_in, b_out, b_in, half_out, half_in,
    a_s, a_r, b_s, b_r, h_s, h_r,
):
    at = lax.axis_index("grp")
    zl = lax.rem(at, 2)
    y = lax.div(at, 2)
    core = lax.rem(lax.axis_index("col"), 2)
    way = 1 - 2 * core

    def ring(step):
        return lax.rem(y + step * way + 2 * Y, Y)

    fwd, back = ring(1) * 2 + zl, ring(-1) * 2 + zl
    mate = y * 2 + (1 - zl)
    panels = own.shape[0]
    greet([("grp", d) for d in (fwd, back, mate)])

    far, near = Y // 2, Y // 2 - 1
    sent = []
    ahead, behind, halves = {}, {}, {}

    def product(p):
        halves_of = [
            shared[p // 2, :, :, p % 2 * 2 + k].reshape(-1, LANE) for k in range(2)
        ]
        right = jnp.concatenate(halves_of, axis=1)
        whole = jnp.dot(turned[...], right, preferred_element_type=jnp.float32)
        own[p] = whole.reshape(own.shape[1:])

    def hop(p, t):
        term = own[p, ring(far - t)]
        if t > 0:
            ahead[p].wait_recv()
            term = term + a_in[p, t - 1].astype(jnp.float32)
        a_out[p, t] = term.astype(jnp.bfloat16)
        ahead[p] = remote(a_out.at[p, t], a_in.at[p, t], a_s.at[p, t], a_r.at[p, t], "grp", fwd)
        sent.append(ahead[p])
        if t < near:
            term = own[p, ring(t - near)]
            if t > 0:
                behind[p].wait_recv()
                term = term + b_in[p, t - 1].astype(jnp.float32)
            b_out[p, t] = term.astype(jnp.bfloat16)
            behind[p] = remote(b_out.at[p, t], b_in.at[p, t], b_s.at[p, t], b_r.at[p, t], "grp", back)
            sent.append(behind[p])

    def meet(p):
        behind[p].wait_recv()
        ahead[p].wait_recv()

        def total(z):
            return (
                own[p, y, z]
                + a_in[p, far - 1, z].astype(jnp.float32)
                + b_in[p, near - 1, z].astype(jnp.float32)
            )

        half_out[p] = total(1 - zl)
        halves[p] = remote(half_out.at[p], half_in.at[p], h_s.at[p], h_r.at[p], "grp", mate)
        sent.append(halves[p])
        out[p] = total(zl)

    def finish(p):
        halves[p].wait_recv()
        out[p] = out[p] + half_in[p]

    for u in range(panels + far + 1):
        if u < panels:
            product(u)
        for p in range(panels):
            t = u - p
            if 0 <= t < far:
                hop(p, t)
            elif t == far:
                meet(p)
            elif t == far + 1:
                finish(p)
    for copy in sent:
        copy.wait_send()


def reduce_over_groups(turned, shared):
    panels, width = 4, 2 * LANE
    rows = turned.shape[0] // (2 * Y)
    block = (2, rows, width)
    far, near = Y // 2, Y // 2 - 1
    f32, bf = jnp.float32, jnp.bfloat16
    dma = pltpu.SemaphoreType.DMA
    vm = pl.BlockSpec(memory_space=pltpu.VMEM)
    return pl.pallas_call(
        reduce_kernel,
        out_shape=jax.ShapeDtypeStruct((panels, rows, width), f32),
        in_specs=[vm, vm],
        out_specs=vm,
        scratch_shapes=[
            pltpu.VMEM((panels, Y) + block, f32),
            pltpu.VMEM((panels, far) + block, bf),
            pltpu.VMEM((panels, far) + block, bf),
            pltpu.VMEM((panels, near) + block, bf),
            pltpu.VMEM((panels, near) + block, bf),
            pltpu.VMEM((panels, rows, width), f32),
            pltpu.VMEM((panels, rows, width), f32),
            dma((panels, far)), dma((panels, far)),
            dma((panels, near)), dma((panels, near)),
            dma((panels,)), dma((panels,)),
        ],
        compiler_params=pltpu.CompilerParams(
            collective_id=1, has_side_effects=True, vmem_limit_bytes=24 * 1024 * 1024
        ),
    )(turned, shared)


def on_device(border, inverses, scen_map, owners, slots):
    shared, turned = share(owners, slots, scen_map, border, inverses)
    return reduce_over_groups(turned, shared)


def solution(mesh):
    return jax.shard_map(
        on_device,
        mesh=mesh,
        in_specs=(P("grp", None, "col"), P("grp", None, None), P("grp", None), P(), P()),
        out_specs=P(None, ("col", "grp"), None),
        check_vma=False,
    )
```

time: 111 us -> 103 us (0.928)
  Pallas kernels: 104 us -> 97 us
    pallas_call x1, Pallas kernels: 64.4 us -> 58.8 us  [share(): pl.pallas_call(share_kernel, out_shape=(jax.ShapeDtypeStruct((2, X) + chu...]
    pallas_call x1, Pallas kernels: 39.8 us -> 38.2 us  [reduce_over_groups(): pl.pallas_call(reduce_kernel, out_shape=jax.ShapeDtypeStruct((panels, row...]
where the time goes in v3:
time: 103 us
  Pallas kernels  97 us (94%)
  local copies, waits for them, and re-layouts  5.58 us (5%)
    pallas_call x1, Pallas kernels, share(): pl.pallas_call(share_kernel, out_shape=(jax.ShapeDtypeStruct((2, X) + chu...  58.8 us
    pallas_call x1, Pallas kernels, reduce_over_groups(): pl.pallas_call(reduce_kernel, out_shape=jax.ShapeDtypeStruct((panels, row...  38.2 us
    unnamed x11, local copies, waits for them, and re-layouts  5.58 us

profile of v3, /device:TPU:6, one launch (start us, length us, event | category | flops | bytes accessed | tf_op | source)
XLA Modules:
  0.0 102.6 jit_solution(9626509291878271788)
XLA Ops:
  0.0 0.0 copy-start
  0.0 1.7 %copy-done = bf16[4,384,768]{2,1,0:T(8,128)(2,1)S(1)} copy-done((bf16[4,384,768]{2,1,0:T(8,128)(2,1)S(1)}, bf16[4,384,768]{2,1,0:T(8,128)(2,1)}, u32[]{:S(2)}) %copy-start) | copy-done | bytes 2359320
  1.7 0.0 copy-start.1
  1.7 1.3 %copy-done.1 = bf16[4,384,384]{2,1,0:T(8,128)(2,1)S(1)} copy-done((bf16[4,384,384]{2,1,0:T(8,128)(2,1)S(1)}, bf16[4,384,384]{2,1,0:T(8,128)(2,1)}, u32[]{:S(2)}) %copy-start.1) | copy-done | bytes 1179672
  2.9 0.0 copy-start.2
  2.9 0.7 copy-done.2
  3.6 0.0 copy-start.3
  3.6 0.7 copy-done.3
  4.2 0.0 copy-start.4
  4.3 0.7 copy-done.4
  4.9 58.8 %shard_map.55 = (bf16[2,4,3,4,128,128]{5,4,3,2,1,0:T(8,128)(2,1)S(1)}, bf16[768,1536]{1,0:T(8,128)(2,1)S(1)}) custom-call(s32[4]{0:T(128)S(1)} %copy-done.2, s32[4]{0:T(128)S(1)} %copy-done.3, s32[1,4]{1,0:T(1,128)S(1)} %copy-done.4, bf16[4,384,768]{2,1,0:T(8,128)(2,1)S(1)} %copy-done, bf16[4,384,384]{2,1,0:T(8,128)(2,1)S(1)} %copy-done.1), custom_call_target="tpu_custom_call" | custom-call | tf_op jit(solution)/shard_map/pallas_call | solution.py:215
  63.7 38.2 %shard_map.56 = f32[4,48,256]{2,1,0:T(8,128)S(1)} custom-call(bf16[768,1536]{1,0:T(8,128)(2,1)S(1)} %get-tuple-element.7.turned, bf16[2,4,3,4,128,128]{5,4,3,2,1,0:T(8,128)(2,1)S(1)} %get-tuple-element.8.shared), custom_call_target="tpu_custom_call" | custom-call | tf_op jit(solution)/shard_map/pallas_call | solution.py:339
  101.9 0.7 copy.7
Async XLA Ops:
  0.0 1.7 %copy-start = (bf16[4,384,768]{2,1,0:T(8,128)(2,1)S(1)}, bf16[4,384,768]{2,1,0:T(8,128)(2,1)}, u32[]{:S(2)}) copy-start(bf16[4,384,768]{2,1,0:T(8,128)(2,1)} %border.1) | copy-start | bytes 7077892
  1.7 1.3 %copy-start.1 = (bf16[4,384,384]{2,1,0:T(8,128)(2,1)S(1)}, bf16[4,384,384]{2,1,0:T(8,128)(2,1)}, u32[]{:S(2)}) copy-start(bf16[4,384,384]{2,1,0:T(8,128)(2,1)} %inverses.1) | copy-start | bytes 3538948
  2.9 0.7 copy-start.2
  3.6 0.7 copy-start.3
  4.2 0.7 copy-start.4

commit v4 on v3

--- a/solution.py
+++ b/solution.py
@@ -1,5 +1,3 @@
-import functools
-
 import jax
 import jax.numpy as jnp
 from jax import lax
@@ -12,6 +10,7 @@
 Y = 8
 LANE = 128
 TILE = 16
+SHARE_REFS = 29
 
 
 def greet(peers):
@@ -36,11 +35,21 @@
     return copy
 
 
-def share_kernel(
-    owners, slots, scen_map, border, inverses, full, turned,
+def share(
+    owners_at, slots_at, scen_map_at, border_at, inverses_at, full, turned, neighbours,
+    owners, slots, scen_map, border, inverses, loads,
     marks, picked, pair_out, pair_in, x_out, x_own, x_in, z_sum, z_in, z_out, home,
     pair_s, pair_r, xs, xr, zs, zr, zgs, zgr, xgs, xgr, bs, br,
 ):
+    fetch = [
+        pltpu.make_async_copy(src, dst, loads.at[k])
+        for k, (src, dst) in enumerate((
+            (owners_at, owners), (slots_at, slots), (scen_map_at, scen_map),
+            (border_at, border), (inverses_at, inverses),
+        ))
+    ]
+    for copy in fetch:
+        copy.start()
     at = lax.axis_index("col")
     core = lax.rem(at, 2)
     zh = lax.rem(lax.div(at, 2), ZH)
@@ -58,10 +67,6 @@
     scen, depth, _ = border.shape
     parts = depth // LANE
     tiles = LANE // TILE
-    for p in range(owners.shape[0]):
-        for k in range(3):
-            marks[p, k] = (flag(owners[p], at) * flag(slots[p], k)).astype(jnp.bfloat16)
-
     def panel(cc, s, r, q):
         total = None
         for k in range(3):
@@ -80,7 +85,14 @@
     partner = col(x, zh, other)
     x_fwd, x_back = col(xa, zh, core), col(xb, zh, core)
     z_fwd, z_back = col(x, za, core), col(x, zb, core)
-    greet([("col", d) for d in (partner, x_fwd, x_back, z_fwd, z_back)])
+    for copy in fetch[:3]:
+        copy.wait()
+    for p in range(owners.shape[0]):
+        for k in range(3):
+            marks[p, k] = (flag(owners[p], at) * flag(slots[p], k)).astype(jnp.bfloat16)
+
+    greet([("col", d) for d in (partner, x_fwd, x_back, z_fwd, z_back)] + neighbours)
+    fetch[3].wait()
 
     order = range(parts)
     sends = []
@@ -119,6 +131,7 @@
         for q in range(ZH):
             x_out[2, r, q] = x_own[0, r, q] + x_in[0, r, q]
         c[2, r] = send(x_out.at[2, r], x_in.at[2, r], xs.at[2, r], xr.at[2, r], "col", x_fwd)
+    fetch[4].wait()
     for lane in range(0, depth, LANE):
         for r in order:
             total = None
@@ -199,28 +212,131 @@
         h[3, r] = pass_on(3, xf, r, bs, br, "col", partner)
     for copy in h.values():
         copy.wait_recv()
+    return sends
+
+
+def group_place():
+    at = lax.axis_index("grp")
+    zl = lax.rem(at, 2)
+    y = lax.div(at, 2)
+    core = lax.rem(lax.axis_index("col"), 2)
+    way = 1 - 2 * core
+
+    def ring(step):
+        return lax.rem(y + step * way + 2 * Y, Y)
+
+    fwd, back = ring(1) * 2 + zl, ring(-1) * 2 + zl
+    mate = y * 2 + (1 - zl)
+    return y, zl, ring, (fwd, back, mate)
+
+
+def reduce(
+    turned, shared, out, sent,
+    own, a_out, a_in, b_out, b_in, half_out, half_in,
+    a_s, a_r, b_s, b_r, h_s, h_r,
+):
+    y, zl, ring, (fwd, back, mate) = group_place()
+    panels = own.shape[0]
+
+    far, near = Y // 2, Y // 2 - 1
+    ahead, behind, halves = {}, {}, {}
+
+    def product(p):
+        halves_of = [
+            shared[p // 2, :, :, p % 2 * 2 + k].reshape(-1, LANE) for k in range(2)
+        ]
+        right = jnp.concatenate(halves_of, axis=1)
+        whole = jnp.dot(turned[...], right, preferred_element_type=jnp.float32)
+        own[p] = whole.reshape(own.shape[1:])
+
+    def hop(p, t):
+        term = own[p, ring(far - t)]
+        if t > 0:
+            ahead[p].wait_recv()
+            term = term + a_in[p, t - 1].astype(jnp.float32)
+        a_out[p, t] = term.astype(jnp.bfloat16)
+        ahead[p] = remote(a_out.at[p, t], a_in.at[p, t], a_s.at[p, t], a_r.at[p, t], "grp", fwd)
+        sent.append(ahead[p])
+        if t < near:
+            term = own[p, ring(t - near)]
+            if t > 0:
+                behind[p].wait_recv()
+                term = term + b_in[p, t - 1].astype(jnp.float32)
+            b_out[p, t] = term.astype(jnp.bfloat16)
+            behind[p] = remote(b_out.at[p, t], b_in.at[p, t], b_s.at[p, t], b_r.at[p, t], "grp", back)
+            sent.append(behind[p])
+
+    def meet(p):
+        behind[p].wait_recv()
+        ahead[p].wait_recv()
+
+        def total(z):
+            return (
+                own[p, y, z]
+                + a_in[p, far - 1, z].astype(jnp.float32)
+                + b_in[p, near - 1, z].astype(jnp.float32)
+            )
+
+        half_out[p] = total(1 - zl)
+        halves[p] = remote(half_out.at[p], half_in.at[p], h_s.at[p], h_r.at[p], "grp", mate)
+        sent.append(halves[p])
+        out[p] = total(zl)
+
+    def finish(p):
+        halves[p].wait_recv()
+        out[p] = out[p] + half_in[p]
+
+    for u in range(panels + far + 1):
+        if u < panels:
+            product(u)
+        for p in reversed(range(panels)):
+            t = u - p
+            if 0 <= t < far:
+                hop(p, t)
+            elif t == far:
+                meet(p)
+            elif t == far + 1:
+                finish(p)
+
+
+def kernel(owners, slots, scen_map, border, inverses, out, full, turned, *scratch):
+    _, _, _, peers = group_place()
+    first = scratch[:SHARE_REFS]
+    sends = share(
+        owners, slots, scen_map, border, inverses, full, turned,
+        [("grp", d) for d in peers], *first
+    )
+    reduce(turned, full, out, sends, *scratch[SHARE_REFS:])
     for copy in sends:
         copy.wait_send()
 
 
-def share(owners, slots, scen_map, border, inverses):
-    scen, depth, rows = border.shape
+def schur(owners, slots, scen_map, border, inverses):
+    scen, depth, cols = border.shape
     parts = depth // LANE
     piece = (parts, LANE, LANE)
     chunk = (parts, ZH, LANE, LANE)
-    bf = jnp.bfloat16
+    panels, width = owners.shape[0], 2 * LANE
+    rows = cols // (2 * Y)
+    block = (2, rows, width)
+    far, near = Y // 2, Y // 2 - 1
+    f32, bf = jnp.float32, jnp.bfloat16
     dma = pltpu.SemaphoreType.DMA
-    vm = pl.BlockSpec(memory_space=pltpu.VMEM)
-    sm = pl.BlockSpec(memory_space=pltpu.SMEM)
+    hbm = pl.BlockSpec(memory_space=pltpu.HBM)
     return pl.pallas_call(
-        share_kernel,
-        out_shape=(
-            jax.ShapeDtypeStruct((2, X) + chunk, bf),
-            jax.ShapeDtypeStruct((rows, scen * depth), bf),
-        ),
-        in_specs=[sm, sm, sm, vm, vm],
-        out_specs=(vm, vm),
+        kernel,
+        out_shape=jax.ShapeDtypeStruct((panels, rows, width), f32),
+        in_specs=[hbm] * 5,
+        out_specs=pl.BlockSpec(memory_space=pltpu.VMEM),
         scratch_shapes=[
+            pltpu.VMEM((2, X) + chunk, bf),
+            pltpu.VMEM((cols, scen * depth), bf),
+            pltpu.SMEM(owners.shape, jnp.int32),
+            pltpu.SMEM(slots.shape, jnp.int32),
+            pltpu.SMEM(scen_map.shape, jnp.int32),
+            pltpu.VMEM(border.shape, bf),
+            pltpu.VMEM(inverses.shape, bf),
+            dma((5,)),
             pltpu.VMEM((4, 3, TILE, LANE), bf),
             pltpu.VMEM((depth, depth), bf),
             pltpu.VMEM((X,) + chunk, bf),
@@ -238,110 +354,6 @@
             dma((3, parts)), dma((3, parts)),
             dma((3, parts)), dma((3, parts)),
             dma((4, parts)), dma((4, parts)),
-        ],
-        compiler_params=pltpu.CompilerParams(
-            collective_id=0, has_side_effects=True, vmem_limit_bytes=24 * 1024 * 1024
-        ),
-    )(owners, slots, scen_map, border, inverses)
-
-
-def reduce_kernel(
-    turned, shared, out,
-    own, a_out, a_in, b_out, b_in, half_out, half_in,
-    a_s, a_r, b_s, b_r, h_s, h_r,
-):
-    at = lax.axis_index("grp")
-    zl = lax.rem(at, 2)
-    y = lax.div(at, 2)
-    core = lax.rem(lax.axis_index("col"), 2)
-    way = 1 - 2 * core
-
-    def ring(step):
-        return lax.rem(y + step * way + 2 * Y, Y)
-
-    fwd, back = ring(1) * 2 + zl, ring(-1) * 2 + zl
-    mate = y * 2 + (1 - zl)
-    panels = own.shape[0]
-    greet([("grp", d) for d in (fwd, back, mate)])
-
-    far, near = Y // 2, Y // 2 - 1
-    sent = []
-    ahead, behind, halves = {}, {}, {}
-
-    def product(p):
-        halves_of = [
-            shared[p // 2, :, :, p % 2 * 2 + k].reshape(-1, LANE) for k in range(2)
-        ]
-        right = jnp.concatenate(halves_of, axis=1)
-        whole = jnp.dot(turned[...], right, preferred_element_type=jnp.float32)
-        own[p] = whole.reshape(own.shape[1:])
-
-    def hop(p, t):
-        term = own[p, ring(far - t)]
-        if t > 0:
-            ahead[p].wait_recv()
-            term = term + a_in[p, t - 1].astype(jnp.float32)
-        a_out[p, t] = term.astype(jnp.bfloat16)
-        ahead[p] = remote(a_out.at[p, t], a_in.at[p, t], a_s.at[p, t], a_r.at[p, t], "grp", fwd)
-        sent.append(ahead[p])
-        if t < near:
-            term = own[p, ring(t - near)]
-            if t > 0:
-                behind[p].wait_recv()
-                term = term + b_in[p, t - 1].astype(jnp.float32)
-            b_out[p, t] = term.astype(jnp.bfloat16)
-            behind[p] = remote(b_out.at[p, t], b_in.at[p, t], b_s.at[p, t], b_r.at[p, t], "grp", back)
-            sent.append(behind[p])
-
-    def meet(p):
-        behind[p].wait_recv()
-        ahead[p].wait_recv()
-
-        def total(z):
-            return (
-                own[p, y, z]
-                + a_in[p, far - 1, z].astype(jnp.float32)
-                + b_in[p, near - 1, z].astype(jnp.float32)
-            )
-
-        half_out[p] = total(1 - zl)
-        halves[p] = remote(half_out.at[p], half_in.at[p], h_s.at[p], h_r.at[p], "grp", mate)
-        sent.append(halves[p])
-        out[p] = total(zl)
-
-    def finish(p):
-        halves[p].wait_recv()
-        out[p] = out[p] + half_in[p]
-
-    for u in range(panels + far + 1):
-        if u < panels:
-            product(u)
-        for p in range(panels):
-            t = u - p
-            if 0 <= t < far:
-                hop(p, t)
-            elif t == far:
-                meet(p)
-            elif t == far + 1:
-                finish(p)
-    for copy in sent:
-        copy.wait_send()
-
-
-def reduce_over_groups(turned, shared):
-    panels, width = 4, 2 * LANE
-    rows = turned.shape[0] // (2 * Y)
-    block = (2, rows, width)
-    far, near = Y // 2, Y // 2 - 1
-    f32, bf = jnp.float32, jnp.bfloat16
-    dma = pltpu.SemaphoreType.DMA
-    vm = pl.BlockSpec(memory_space=pltpu.VMEM)
-    return pl.pallas_call(
-        reduce_kernel,
-        out_shape=jax.ShapeDtypeStruct((panels, rows, width), f32),
-        in_specs=[vm, vm],
-        out_specs=vm,
-        scratch_shapes=[
             pltpu.VMEM((panels, Y) + block, f32),
             pltpu.VMEM((panels, far) + block, bf),
             pltpu.VMEM((panels, far) + block, bf),
@@ -354,14 +366,13 @@
             dma((panels,)), dma((panels,)),
         ],
         compiler_params=pltpu.CompilerParams(
-            collective_id=1, has_side_effects=True, vmem_limit_bytes=24 * 1024 * 1024
+            collective_id=0, has_side_effects=True, vmem_limit_bytes=64000 * 1024
         ),
-    )(turned, shared)
+    )(owners, slots, scen_map, border, inverses)
 
 
 def on_device(border, inverses, scen_map, owners, slots):
-    shared, turned = share(owners, slots, scen_map, border, inverses)
-    return reduce_over_groups(turned, shared)
+    return schur(owners, slots, scen_map, border, inverses)
 
 
 def solution(mesh):

time: 103 us -> 91.5 us (0.89)
  Pallas kernels: 97 us -> 89.3 us
  local copies, waits for them, and re-layouts: 5.58 us -> 1.62 us
    pallas_call x2 -> x1, Pallas kernels: 97 us -> 89.3 us  [schur(): pl.pallas_call(kernel, out_shape=jax.ShapeDtypeStruct((panels, rows, widt...]
    unnamed x11 -> x1, local copies, waits for them, and re-layouts: 5.58 us -> 1.62 us
where the time goes in v4:
time: 91.5 us; the launch traced here: 90.9 us
  Pallas kernels  89.3 us (98%)
  local copies, waits for them, and re-layouts  1.62 us (2%)
    pallas_call x1, Pallas kernels, schur(): pl.pallas_call(kernel, out_shape=jax.ShapeDtypeStruct((panels, rows, widt...  89.3 us

profile of v4, /device:TPU:6, one launch (start us, length us, event | category | flops | bytes accessed | tf_op | source)
XLA Modules:
  0.0 90.9 jit_solution(1213283485822354394)
XLA Ops:
  0.0 89.3 %shard_map.55 = f32[4,48,256]{2,1,0:T(8,128)} custom-call(s32[4]{0:T(128)} %owners.1, s32[4]{0:T(128)} %slots.1, s32[1,4]{1,0:T(1,128)} %scen_map.1, bf16[4,384,768]{2,1,0:T(8,128)(2,1)} %border.1, bf16[4,384,384]{2,1,0:T(8,128)(2,1)} %inverses.1), custom_call_target="tpu_custom_call" | custom-call | tf_op jit(solution)/shard_map/pallas_call | solution.py:326
  89.3 1.6 %copy.7 = f32[4,48,256]{2,1,0:T(8,128)} copy(f32[4,48,256]{2,1,0:T(8,128)} %shard_map.55) | data formatting | bytes 393216

commit v5 on v4

--- a/solution.py
+++ b/solution.py
@@ -184,35 +184,55 @@
             )
         full[core, x, r, zh] = home[r]
 
-    def pass_on(k, s, r, sent, got, axis, peer):
-        return send(full.at[core, s, r], full.at[core, s, r], sent.at[k, r], got.at[k, r], axis, peer)
-
+    g, h = {}, {}
+
+    def pass_on(kept, k, s, i, r, sent, got, peer):
+        held = full.at[core, s, r, 2 * i:2 * i + 2]
+        kept[k, i, r] = send(held, held, sent.at[k, i, r], got.at[k, i, r], "col", peer)
+
+    def to_partner(k, s, i, r):
+        pass_on(h, k, s, i, r, bs, br, partner)
+
+    def spread_own(i, r):
+        pass_on(g, 0, x, i, r, xgs, xgr, x_fwd)
+        pass_on(g, 1, x, i, r, xgs, xgr, x_back)
+        to_partner(0, x, i, r)
+
+    def take_back(i):
+        for r in order:
+            g[0, i, r].wait_recv()
+            pass_on(g, 2, xb, i, r, xgs, xgr, x_fwd)
+            to_partner(1, xb, i, r)
+
+    def take_fwd(i):
+        for r in order:
+            g[1, i, r].wait_recv()
+            to_partner(2, xa, i, r)
+
+    def take_far(i):
+        for r in order:
+            g[2, i, r].wait_recv()
+            to_partner(3, xf, i, r)
+        for k in range(X):
+            for r in order:
+                h[k, i, r].wait_recv()
+
+    turn(2)
     for r in order:
         e[0, r].wait_recv()
         held = full.at[core, x, r, zb]
         e[2, r] = send(held, held, zgs.at[2, r], zgr.at[2, r], "col", z_fwd)
-    g, h = {}, {}
     for r in order:
         e[1, r].wait_recv()
         e[2, r].wait_recv()
-        g[0, r] = pass_on(0, x, r, xgs, xgr, "col", x_fwd)
-        g[1, r] = pass_on(1, x, r, xgs, xgr, "col", x_back)
-        h[0, r] = pass_on(0, x, r, bs, br, "col", partner)
-    turn(2)
-    for r in order:
-        g[0, r].wait_recv()
-        g[2, r] = pass_on(2, xb, r, xgs, xgr, "col", x_fwd)
-        h[1, r] = pass_on(1, xb, r, bs, br, "col", partner)
+        spread_own(0, r)
+    take_back(0)
+    for r in order:
+        spread_own(1, r)
     turn(3)
-    for r in order:
-        g[1, r].wait_recv()
-        h[2, r] = pass_on(2, xa, r, bs, br, "col", partner)
-    for r in order:
-        g[2, r].wait_recv()
-        h[3, r] = pass_on(3, xf, r, bs, br, "col", partner)
-    for copy in h.values():
-        copy.wait_recv()
-    return sends
+    take_fwd(0)
+    take_far(0)
+    return sends, {1: take_back, 2: take_fwd, 3: take_far}
 
 
 def group_place():
@@ -231,7 +251,7 @@
 
 
 def reduce(
-    turned, shared, out, sent,
+    turned, shared, out, sent, before,
     own, a_out, a_in, b_out, b_in, half_out, half_in,
     a_s, a_r, b_s, b_r, h_s, h_r,
 ):
@@ -286,11 +306,14 @@
         halves[p].wait_recv()
         out[p] = out[p] + half_in[p]
 
-    for u in range(panels + far + 1):
-        if u < panels:
-            product(u)
-        for p in reversed(range(panels)):
-            t = u - p
+    starts = {0: 0, 2: 1, 1: 3, 3: 4}
+    for u in range(max(starts.values()) + far + 2):
+        if u in before:
+            before[u](1)
+        for p in reversed((0, 2, 1, 3)):
+            t = u - starts[p]
+            if t == 0:
+                product(p)
             if 0 <= t < far:
                 hop(p, t)
             elif t == far:
@@ -302,11 +325,11 @@
 def kernel(owners, slots, scen_map, border, inverses, out, full, turned, *scratch):
     _, _, _, peers = group_place()
     first = scratch[:SHARE_REFS]
-    sends = share(
+    sends, later = share(
         owners, slots, scen_map, border, inverses, full, turned,
         [("grp", d) for d in peers], *first
     )
-    reduce(turned, full, out, sends, *scratch[SHARE_REFS:])
+    reduce(turned, full, out, sends, later, *scratch[SHARE_REFS:])
     for copy in sends:
         copy.wait_send()
 
@@ -352,8 +375,8 @@
             dma((3, parts)), dma((3, parts)),
             dma((3, parts)), dma((3, parts)),
             dma((3, parts)), dma((3, parts)),
-            dma((3, parts)), dma((3, parts)),
-            dma((4, parts)), dma((4, parts)),
+            dma((3, 2, parts)), dma((3, 2, parts)),
+            dma((4, 2, parts)), dma((4, 2, parts)),
             pltpu.VMEM((panels, Y) + block, f32),
             pltpu.VMEM((panels, far) + block, bf),
             pltpu.VMEM((panels, far) + block, bf),

time: 91.5 us -> 92.6 us (1.012)
  the two profiles are of different devices: /device:TPU:6 before, /device:TPU:2 now
where the time goes in v5:
time: 92.6 us; the launch traced here: 92.4 us
  Pallas kernels  90.8 us (98%)
  local copies, waits for them, and re-layouts  1.62 us (2%)
    pallas_call x1, Pallas kernels, schur(): pl.pallas_call(kernel, out_shape=jax.ShapeDtypeStruct((panels, rows, widt...  90.8 us

profile of v5, /device:TPU:2, one launch (start us, length us, event | category | flops | bytes accessed | tf_op | source)
XLA Modules:
  0.0 92.4 jit_solution(11998711815760687150)
XLA Ops:
  0.0 90.8 %shard_map.55 = f32[4,48,256]{2,1,0:T(8,128)} custom-call(s32[4]{0:T(128)} %owners.1, s32[4]{0:T(128)} %slots.1, s32[1,4]{1,0:T(1,128)} %scen_map.1, bf16[4,384,768]{2,1,0:T(8,128)(2,1)} %border.1, bf16[4,384,384]{2,1,0:T(8,128)(2,1)} %inverses.1), custom_call_target="tpu_custom_call" | custom-call | tf_op jit(solution)/shard_map/pallas_call | solution.py:349
  90.8 1.6 %copy.7 = f32[4,48,256]{2,1,0:T(8,128)} copy(f32[4,48,256]{2,1,0:T(8,128)} %shard_map.55) | data formatting | bytes 393216

commit v6 on v4

--- a/solution.py
+++ b/solution.py
@@ -103,7 +103,8 @@
         return copy
 
     pair = {}
-    for k, s in enumerate((xf, xa, xb, x)):
+
+    def give(k, s):
         for r in order:
             for q in range(ZH):
                 pair_out[k, r, q] = panel(other, s, r, q)
@@ -115,12 +116,20 @@
         return panel(core, s, r, q) + pair_in[s, r, q]
 
     c = {}
-    for k, s, peer in ((0, xf, x_fwd), (1, xb, x_back)):
+
+    def take(k, s, peer):
         for r in order:
             pair[k, r].wait_recv()
             for q in range(ZH):
                 x_out[k, r, q] = joined(k, s, r, q)
             c[k, r] = send(x_out.at[k, r], x_in.at[k, r], xs.at[k, r], xr.at[k, r], "col", peer)
+
+    give(0, xf)
+    give(1, xa)
+    take(0, xf, x_fwd)
+    give(2, xb)
+    take(1, xb, x_back)
+    give(3, x)
     for r in order:
         pair[2, r].wait_recv()
         for q in range(ZH):
@@ -187,6 +196,7 @@
     def pass_on(k, s, r, sent, got, axis, peer):
         return send(full.at[core, s, r], full.at[core, s, r], sent.at[k, r], got.at[k, r], axis, peer)
 
+    turn(2)
     for r in order:
         e[0, r].wait_recv()
         held = full.at[core, x, r, zb]
@@ -198,7 +208,6 @@
         g[0, r] = pass_on(0, x, r, xgs, xgr, "col", x_fwd)
         g[1, r] = pass_on(1, x, r, xgs, xgr, "col", x_back)
         h[0, r] = pass_on(0, x, r, bs, br, "col", partner)
-    turn(2)
     for r in order:
         g[0, r].wait_recv()
         g[2, r] = pass_on(2, xb, r, xgs, xgr, "col", x_fwd)
@@ -289,7 +298,7 @@
     for u in range(panels + far + 1):
         if u < panels:
             product(u)
-        for p in reversed(range(panels)):
+        for p in ([u] if u < panels else []) + list(range(min(u, panels))):
             t = u - p
             if 0 <= t < far:
                 hop(p, t)

time: 91.5 us -> 96.6 us (1.056)
  Pallas kernels: 89.3 us -> 94.8 us
    pallas_call x1, Pallas kernels: 89.3 us -> 94.8 us  [schur(): pl.pallas_call(kernel, out_shape=jax.ShapeDtypeStruct((panels, rows, widt...]
where the time goes in v6:
time: 96.6 us; the launch traced here: 96.5 us
  Pallas kernels  94.8 us (98%)
  local copies, waits for them, and re-layouts  1.62 us (2%)
    pallas_call x1, Pallas kernels, schur(): pl.pallas_call(kernel, out_shape=jax.ShapeDtypeStruct((panels, rows, widt...  94.8 us

profile of v6, /device:TPU:6, one launch (start us, length us, event | category | flops | bytes accessed | tf_op | source)
XLA Modules:
  0.0 96.5 jit_solution(10329010430577943927)
XLA Ops:
  0.0 94.8 %shard_map.55 = f32[4,48,256]{2,1,0:T(8,128)} custom-call(s32[4]{0:T(128)} %owners.1, s32[4]{0:T(128)} %slots.1, s32[1,4]{1,0:T(1,128)} %scen_map.1, bf16[4,384,768]{2,1,0:T(8,128)(2,1)} %border.1, bf16[4,384,384]{2,1,0:T(8,128)(2,1)} %inverses.1), custom_call_target="tpu_custom_call" | custom-call | tf_op jit(solution)/shard_map/pallas_call | solution.py:335
  94.9 1.6 %copy.7 = f32[4,48,256]{2,1,0:T(8,128)} copy(f32[4,48,256]{2,1,0:T(8,128)} %shard_map.55) | data formatting | bytes 393216

commit v7 on v5

--- a/solution.py
+++ b/solution.py
@@ -217,7 +217,6 @@
             for r in order:
                 h[k, i, r].wait_recv()
 
-    turn(2)
     for r in order:
         e[0, r].wait_recv()
         held = full.at[core, x, r, zb]
@@ -229,6 +228,7 @@
     take_back(0)
     for r in order:
         spread_own(1, r)
+    turn(2)
     turn(3)
     take_fwd(0)
     take_far(0)

time: 92.6 us -> 92.6 us (level)
  no operation moved by 1% of the time
where the time goes in v7:
time: 92.6 us; the launch traced here: 92.4 us
  Pallas kernels  90.8 us (98%)
  local copies, waits for them, and re-layouts  1.62 us (2%)
    pallas_call x1, Pallas kernels, schur(): pl.pallas_call(kernel, out_shape=jax.ShapeDtypeStruct((panels, rows, widt...  90.8 us

profile of v7, /device:TPU:2, one launch (start us, length us, event | category | flops | bytes accessed | tf_op | source)
XLA Modules:
  0.0 92.4 jit_solution(3193091351162665646)
XLA Ops:
  0.0 90.8 %shard_map.55 = f32[4,48,256]{2,1,0:T(8,128)} custom-call(s32[4]{0:T(128)} %owners.1, s32[4]{0:T(128)} %slots.1, s32[1,4]{1,0:T(1,128)} %scen_map.1, bf16[4,384,768]{2,1,0:T(8,128)(2,1)} %border.1, bf16[4,384,384]{2,1,0:T(8,128)(2,1)} %inverses.1), custom_call_target="tpu_custom_call" | custom-call | tf_op jit(solution)/shard_map/pallas_call | solution.py:349
  90.8 1.6 %copy.7 = f32[4,48,256]{2,1,0:T(8,128)} copy(f32[4,48,256]{2,1,0:T(8,128)} %shard_map.55) | data formatting | bytes 393216
